TPU v7x, 32 devices: a whole 2x2x4 slice. The times are simulated.
32 devices in a mesh: groups: 2 (over x), wide: 4 (over y, core), pair: 4 (over z).
Axes of the slice: x: 2, y: 2, z: 4, core: 2. Of those that a mesh axis runs over, the one named last changes fastest.
Arguments:
- strips: bfloat16 [8, 2, 4096, 256], P(('groups', 'wide'), None, 'pair'), parts along dimension 0, may hold values from -80 to 80
- offsets: int32 [16, 4, 2], P('groups'), parts along dimension 0, may hold values from 0 to 3328, as said below
- block_subgrid: int32 [64], P(('groups', 'wide', 'pair')), parts along dimension 0, may hold values from 0 to 1
- block_kernel: int32 [64, 2], P(('groups', 'wide', 'pair')), parts along dimension 0, may hold values from 0 to 15
- vis_cells: int32 [64, 2, 2048], P(('groups', 'wide', 'pair')), parts along dimension 0, may hold values from 0 to 248
Outputs:
- predicted: float32 [64, 2, 2048], P(('groups', 'wide', 'pair')), parts along dimension 0
There are 2 independent parts, one for each index of `groups`. A program takes and returns all parts, laid end to end along the dimension named above; each array names one. Nothing has to cross between parts.
Inputs may be any that keep to these rules, and one draw needn't show every extreme that they name: offsets[..., 0] lies in 0 to 3328 and offsets[..., 1] in 0 to 255; both ends of both ranges occur.
All inputs are finite; a program needn't handle non-finite values.
Results may differ from a plain program's by a relative error of at most 0.0033.
The roundings to bfloat16 on the way count: a program that leaves them out, or rounds other values in their place, can miss the bound.
Values may be sent and summed in bfloat16 or wider, within the bound.
No kernel may reach another device: no remote copies, remote signals or barrier semaphores. Data moves between devices by JAX's collectives and lax.ppermute only.
A program may use at most 64 MiB of HBM per device.

v0:
```python
import math
import jax
import jax.numpy as jnp
from jax import lax
from jax.sharding import PartitionSpec as P

L = 4096
SUBW = 256
NVIS = 2048
SUPPORT = 8
OVERSAMPLE = 16
SG_WIDE = 2


def strip_block(row_ids, shift, row_index, length):
    frequency = row_ids - SUBW // 2 + shift
    product = frequency[:, None] * row_index[None, :] % length
    phase_arg = 2.0 * math.pi / length * product.astype(jnp.float32)
    centred = (2 * row_index + 1).astype(jnp.float32) / length - 1.0
    taper = (1.0 - 0.5 * centred * centred) / math.sqrt(length)
    cosine = jnp.cos(phase_arg) * taper[None, :]
    sine = jnp.sin(phase_arg) * taper[None, :]
    upper = jnp.concatenate([cosine, sine], axis=1)
    lower = jnp.concatenate([-sine, cosine], axis=1)
    return jnp.concatenate([upper, lower], axis=0).astype(jnp.bfloat16)


def column_ramp(stacked, shift):
    half = stacked.shape[0] // 2
    part_re = stacked[:half]
    part_im = stacked[half:]
    column_ids = jnp.arange(SUBW, dtype=jnp.int32)
    phase_arg = 2.0 * math.pi / SUBW * (shift * column_ids % SUBW).astype(jnp.float32)
    cosine = jnp.cos(phase_arg)[None, :]
    sine = jnp.sin(phase_arg)[None, :]
    out_re = part_re * cosine + part_im * sine
    out_im = part_im * cosine - part_re * sine
    return jnp.concatenate([out_re, out_im], axis=1)


def transform_table():
    grid_ids = jnp.arange(SUBW, dtype=jnp.int32)
    phase_arg = (
        2.0 * math.pi / SUBW * (grid_ids[:, None] * grid_ids[None, :] % SUBW).astype(jnp.float32)
    )
    cosine = jnp.cos(phase_arg) / math.sqrt(SUBW)
    sine = jnp.sin(phase_arg) / math.sqrt(SUBW)
    upper = jnp.concatenate([cosine, -sine], axis=1)
    lower = jnp.concatenate([sine, cosine], axis=1)
    return jnp.concatenate([upper, lower], axis=0).astype(jnp.bfloat16)


def kernel_taps(fraction):
    points = jnp.arange(SUPPORT, dtype=jnp.float32)
    centre = (SUPPORT - 1) / 2.0 + (fraction.astype(jnp.float32) + 0.5) / OVERSAMPLE - 0.5
    distance = points[None, :] - centre[:, None]
    values = jnp.exp(-distance * distance / 2.88)
    return values / jnp.sum(values, axis=-1, keepdims=True)


def column_sum(spread_rows, col_ids, col_taps):
    columns = jnp.arange(SUBW, dtype=jnp.int32)
    distance = columns[None, None, :] - col_ids[:, :, None]
    weights = jnp.zeros(distance.shape, jnp.float32)
    for tap_index in range(SUPPORT):
        weight = col_taps[:, tap_index][:, None, None]
        weights = jnp.where(distance == tap_index, weight, weights)
    real_part = jnp.sum(weights * spread_rows[..., :SUBW], axis=-1)
    imag_part = jnp.sum(weights * spread_rows[..., SUBW:], axis=-1)
    return jnp.stack([real_part, imag_part], axis=-2)


def on_device(strips, offsets, block_subgrid, block_kernel, vis_cells):
    pair_count = lax.axis_size("pair")
    facet_id = lax.axis_index("wide")
    pair_id = lax.axis_index("pair")
    rows_dev = SG_WIDE * SUBW // pair_count
    local_rows = strips.shape[2]
    xstack = strips.reshape(2 * local_rows, SUBW)
    row_index = pair_id * local_rows + jnp.arange(local_rows, dtype=jnp.int32)

    def single(block_no):
        first = block_no * rows_dev
        subgrid_id = first // SUBW
        row_ids = first % SUBW + jnp.arange(rows_dev, dtype=jnp.int32)
        factor = strip_block(row_ids, offsets[subgrid_id, facet_id, 0], row_index, L)
        product = jnp.dot(factor, xstack, preferred_element_type=jnp.float32)
        return column_ramp(product, offsets[subgrid_id, facet_id, 1])

    stacked = lax.map(
        single, jnp.arange(rows_dev * lax.axis_size(("wide", "pair")) // rows_dev, dtype=jnp.int32)
    )
    summed = lax.psum_scatter(
        stacked.reshape(rows_dev * lax.axis_size(("wide", "pair")), 2 * SUBW),
        ("wide", "pair"),
        scatter_dimension=0,
        tiled=True,
    )
    subgrid = summed.astype(jnp.bfloat16)
    spectrum = jnp.dot(subgrid, transform_table(), preferred_element_type=jnp.float32).astype(
        jnp.bfloat16
    )
    blocks = vis_cells.shape[0]
    row_taps = kernel_taps(block_kernel[:, 0]).astype(jnp.bfloat16)
    col_taps = kernel_taps(block_kernel[:, 1])
    row_base = block_subgrid[:, None] * SUBW + vis_cells[:, 0, :]
    portion = lax.all_gather(spectrum, "pair", axis=0, tiled=True)
    amount = portion.shape[0]
    row_ids = jnp.arange(amount, dtype=jnp.int32)
    distance = row_ids[None, None, :] - row_base[:, :, None]
    dense = jnp.zeros(distance.shape, jnp.float32)
    for tap_index in range(SUPPORT):
        weight = row_taps[:, tap_index].astype(jnp.float32)[:, None, None]
        dense = jnp.where(distance == tap_index, weight, dense)
    dense = dense.astype(jnp.bfloat16).reshape(blocks * NVIS, amount)
    gathered = jnp.dot(dense, portion, preferred_element_type=jnp.float32)
    spread = gathered.reshape(blocks, NVIS, 2 * SUBW)
    return column_sum(spread, vis_cells[:, 1, :], col_taps)


def solution(mesh):
    placed = (
        P(("groups", "wide"), None, "pair", None),
        P("groups", None, None),
        P(("groups", "wide", "pair")),
        P(("groups", "wide", "pair"), None),
        P(("groups", "wide", "pair"), None, None),
    )
    return jax.shard_map(
        on_device,
        mesh=mesh,
        in_specs=placed,
        out_specs=P(("groups", "wide", "pair"), None, None),
        check_vma=False,
    )
```

profile of v0, /device:TPU:0, one launch (start us, length us, event | category | flops | bytes accessed | tf_op | source)
XLA Modules:
  0.0 266.4 jit_solution(9362500942435788892)
XLA Ops:
  6.5 151.5 %while.14 = (s32[]{:T(128)}, f32[16,128,512]{2,1,0:T(8,128)}, s32[16]{0:T(128)S(1)}, s32[8,4,2]{0,2,1:T(2,128)}, s32[]{:T(128)}, /*index=5*/bf16[2048,256]{1,0:T...) while((s32[]{:T(128)}, f32[16,128,512]{2,1,0:T(8,128)}, ...), condition=%wide.region_3.4_spmd.clone, body=%wide.region_2.3_spmd.clone.sunk | while | flops 275528608 | bytes 5003174 | solution.py:90
  10.0 2.5 fusion.103
  12.4 1.8 fusion.104
  19.4 2.5 fusion.103
  28.9 2.5 fusion.103
  31.4 1.8 fusion.104
  38.3 2.5 fusion.103
  47.8 2.5 fusion.103
  57.3 2.5 fusion.103
  66.8 2.5 fusion.103
  76.2 2.5 fusion.103
  78.7 1.8 fusion.104
  85.7 2.5 fusion.103
  95.2 2.5 fusion.103
  104.6 2.5 fusion.103
  114.1 2.5 fusion.103
  123.6 2.5 fusion.103
  133.0 2.5 fusion.103
  142.5 2.5 fusion.103
  152.0 2.5 fusion.103
  161.4 72.2 %reduce-scatter.2.cloned.1.call-done = f32[128,512]{1,0:T(8,128)} async-done(((f32[2048,512]{1,0:T(8,128)}), f32[128,512]{1,0:T(8,128)}) %reduce-scatter.2.cloned.1.call-update) | async-done | bytes 262160 | tf_op jit(solution)/shard_map/reduce_scatter | solution.py:93
  234.8 14.9 %all_gather.3 = bf16[512,512]{0,1:T(8,128)(2,1)S(1)} all-gather(bf16[128,512]{0,1:T(8,128)(2,1)S(1)} %convolution_convert_fusion), channel_id=1, replica_groups=mesh['groups'=2,'wide'=4,'pair'=4] {'pair'}, dimensions={0}, use_global_device_ids=true | all-gather | bytes 655360 | tf_op jit(solution)/shard_map/all_gather | solution.py:107
  249.7 6.0 %fusion.30 = f32[2,2048,512]{1,2,0:T(8,128)S(1)} fusion(bf16[2]{0:T(256)(128)(2,1)S(1)} %get-tuple-element.198, bf16[2]{0:T(256)(128)(2,1)S(1)} %get-tuple-element.199, bf16[2]{0:T(256)(128)(2,1)S(1)} %get-tuple-element.200, bf16[2]{0:T(256)(128)(2,1)S(1)} %get-tuple-element.201, bf16[2]{0:T(256)(128)(2,1)S(1)} %get-tuple-element.202, ...), kind=kOutput, calls=%fused_computation.51 | convolution fusion | flops 2183135232 | bytes 8929312 | tf_op jit(solution)/shard_map/dot_general | solution.py:116
  255.7 3.2 %fusion.32 = (f32[2,2048]{1,0:T(2,128)S(1)}, f32[2,2048]{1,0:T(2,128)S(1)}) fusion(f32[2,2048,512]{1,2,0:T(8,128)S(1)} %fusion.30, f32[2]{0:T(128)S(1)} %get-tuple-element.190, f32[2]{0:T(128)S(1)} %get-tuple-element.191, f32[2]{0:T(128)S(1)} %get-tuple-element.192, f32[2]{0:T(128)S(1)} %get-tuple-element.193, f32[2]{0:T(128)S(1)} %get-tuple-element.194, ...), kind=kLoop, calls=%fused_computation.55 | loop fusion | flops 22011904 | bytes 8437824 | tf_op jit(solution)/shard_map/reduce_sum | solution.py:68
  (198 shorter events, 99.2 us)
Async XLA Ops:
  6.5 227.0 %reduce-scatter.2.cloned.1.call-start = ((), (), s32[]{:S(2)}) async-start(), calls=%async_computation.1 | async-start | bytes 4456448 | tf_op jit(solution)/shard_map/reduce_scatter | solution.py:93
  158.0 0.8 copy-start
  158.0 0.8 copy-start.1
  158.0 3.2 %copy-start.2 = (s32[2]{0:T(128)S(1)}, s32[2]{0:T(128)}, u32[]{:S(2)}) copy-start(s32[2]{0:T(128)} %param.9) | copy-start | bytes 28
Sparse Core Ops, SparseCore 0:
  158.2 75.2 reduce-scatter.1
where the time goes:
time: 268 us; the launch traced here: 266 us
  waiting for transfers between devices  72.2 us (27%)
  other arithmetic  69.1 us (26%)
  local copies, waits for them, and re-layouts  48.5 us (18%)
  matrix products  35.7 us (13%)
  blocking collectives  14.9 us (6%)
  between operations  13.5 us (5%)
  loops' own time  12.6 us (5%)
    reduce_scatter x1, waiting for transfers between devices, on_device(): lax.psum_scatter(stacked.reshape(rows_dev * lax.axis_size(('wide', 'pair'...  72.2 us
    another operation x18, other arithmetic  41.8 us
    dot_general x16, matrix products, single(): product = jnp.dot(factor, xstack, preferred_element_type=jnp.float32)  28.4 us
    dynamic_slice x16, local copies, waits for them, and re-layouts, single(): return column_ramp(product, offsets[subgrid_id, facet_id, 1])  22.8 us
    all_gather x1, blocking collectives, on_device(): portion = lax.all_gather(spectrum, 'pair', axis=0, tiled=True)  14.9 us
    dynamic_update_slice x32, local copies, waits for them, and re-layouts, on_device(): lax.map(single, jnp.arange(rows_dev * lax.axis_size(('wide', 'pair')) //...  13.8 us
    another operation x1, loops' own time, on_device(): lax.map(single, jnp.arange(rows_dev * lax.axis_size(('wide', 'pair')) //...  12.6 us
    sin x16, other arithmetic, column_ramp(): sine = jnp.sin(phase_arg)[None, :]  11.8 us
  transfers between devices with their start and end apart: 1, of which 1 were waited for; matrix products, arithmetic and copies ran while one was open for 1% of the time, Pallas kernels for 0%

commit v1 on v0

--- a/solution.py
+++ b/solution.py
@@ -104,7 +104,15 @@
     row_taps = kernel_taps(block_kernel[:, 0]).astype(jnp.bfloat16)
     col_taps = kernel_taps(block_kernel[:, 1])
     row_base = block_subgrid[:, None] * SUBW + vis_cells[:, 0, :]
-    portion = lax.all_gather(spectrum, "pair", axis=0, tiled=True)
+    portion = jnp.concatenate(
+        lax.all_to_all(
+            jnp.stack(lax.axis_size("pair") * [spectrum], axis=0),
+            "pair",
+            split_axis=0,
+            concat_axis=0,
+        ),
+        axis=0,
+    )
     amount = portion.shape[0]
     row_ids = jnp.arange(amount, dtype=jnp.int32)
     distance = row_ids[None, None, :] - row_base[:, :, None]

time: 268 us -> 271 us (1.011)
  blocking collectives: 14.9 us -> 0 us
  waiting for transfers between devices: 72.2 us -> 85.1 us
  starting transfers between devices: 0.01 us -> 3.47 us
    all_gather x1 -> x0, blocking collectives: 14.9 us -> none  [on_device(): portion = lax.all_gather(spectrum, 'pair', axis=0, tiled=True)]
    all_to_all x0 -> x1, waiting for transfers between devices: none -> 12.9 us  [on_device(): lax.all_to_all(jnp.stack(lax.axis_size('pair') * [spectrum], axis=0), 'pa...]
    all_to_all x0 -> x1, starting transfers between devices: none -> 3.47 us  [on_device(): lax.all_to_all(jnp.stack(lax.axis_size('pair') * [spectrum], axis=0), 'pa...]
  transfers between devices with their start and end apart: 1 -> 2, of which waited for: 1 -> 2; matrix products, arithmetic and copies ran while one was open for 1% -> 1% of each run, Pallas kernels for 0% -> 0%
where the time goes in v1:
time: 271 us; the launch traced here: 269 us
  waiting for transfers between devices  85.1 us (31%)
  other arithmetic  69.1 us (25%)
  local copies, waits for them, and re-layouts  50.1 us (18%)
  matrix products  35.6 us (13%)
  between operations  13.5 us (5%)
  loops' own time  12.6 us (5%)
  starting transfers between devices  3.47 us (1%)
    reduce_scatter x1, waiting for transfers between devices, on_device(): lax.psum_scatter(stacked.reshape(rows_dev * lax.axis_size(('wide', 'pair'...  72.3 us
    another operation x18, other arithmetic  41.8 us
    dot_general x16, matrix products, single(): product = jnp.dot(factor, xstack, preferred_element_type=jnp.float32)  28.4 us
    dynamic_slice x16, local copies, waits for them, and re-layouts, single(): return column_ramp(product, offsets[subgrid_id, facet_id, 1])  22.8 us
    dynamic_update_slice x32, local copies, waits for them, and re-layouts, on_device(): lax.map(single, jnp.arange(rows_dev * lax.axis_size(('wide', 'pair')) //...  13.8 us
    all_to_all x1, waiting for transfers between devices, on_device(): lax.all_to_all(jnp.stack(lax.axis_size('pair') * [spectrum], axis=0), 'pa...  12.9 us
    another operation x1, loops' own time, on_device(): lax.map(single, jnp.arange(rows_dev * lax.axis_size(('wide', 'pair')) //...  12.6 us
    sin x16, other arithmetic, column_ramp(): sine = jnp.sin(phase_arg)[None, :]  11.8 us
  transfers between devices with their start and end apart: 2, of which 2 were waited for; matrix products, arithmetic and copies ran while one was open for 1% of the time, Pallas kernels for 0%

profile of v1, /device:TPU:0, one launch (start us, length us, event | category | flops | bytes accessed | tf_op | source)
XLA Modules:
  0.0 269.5 jit_solution(12594517341160464986)
XLA Ops:
  6.5 151.5 %while.14 = (s32[]{:T(128)}, f32[16,128,512]{2,1,0:T(8,128)}, s32[16]{0:T(128)S(1)}, s32[8,4,2]{0,2,1:T(2,128)}, s32[]{:T(128)}, /*index=5*/bf16[2048,256]{1,0:T...) while((s32[]{:T(128)}, f32[16,128,512]{2,1,0:T(8,128)}, ...), condition=%wide.region_3.4_spmd.clone, body=%wide.region_2.3_spmd.clone.sunk | while | flops 275528608 | bytes 5003174 | solution.py:90
  10.0 2.5 fusion.105
  12.4 1.8 fusion.106
  19.4 2.5 fusion.105
  28.9 2.5 fusion.105
  38.3 2.5 fusion.105
  47.8 2.5 fusion.105
  57.3 2.5 fusion.105
  66.8 2.5 fusion.105
  76.2 2.5 fusion.105
  78.7 1.8 fusion.106
  85.7 2.5 fusion.105
  95.2 2.5 fusion.105
  104.6 2.5 fusion.105
  114.1 2.5 fusion.105
  123.6 2.5 fusion.105
  133.0 2.5 fusion.105
  142.5 2.5 fusion.105
  152.0 2.5 fusion.105
  161.2 72.3 %reduce-scatter.2.cloned.1.call-done = f32[128,512]{1,0:T(8,128)} async-done(((f32[2048,512]{1,0:T(8,128)}), f32[128,512]{1,0:T(8,128)}) %reduce-scatter.2.cloned.1.call-update) | async-done | bytes 262160 | tf_op jit(solution)/shard_map/reduce_scatter | solution.py:93
  235.7 3.5 %all-to-all-start = ((bf16[4,128,512]{1,2,0:T(8,128)(2,1)}), bf16[4,128,512]{1,2,0:T(8,128)(2,1)S(1)}, u32[]{:S(2)}, u32[]{:S(2)}) async-start(bf16[4,128,512]{1,2,0:T(8,128)(2,1)} %stack.16), calls=%async_computation.1 | async-start | bytes 1048576 | tf_op jit(solution)/shard_map/all_to_all | solution.py:108
  239.3 12.9 %all-to-all-done = bf16[4,128,512]{1,2,0:T(8,128)(2,1)S(1)} async-done(((bf16[4,128,512]{1,2,0:T(8,128)(2,1)}), bf16[4,128,512]{1,2,0:T(8,128)(2,1)S(1)}, u32[]{:S(2)}, u32[]{:S(2)}) %all-to-all-start) | async-done | bytes 524320 | tf_op jit(solution)/shard_map/all_to_all | solution.py:108
  252.8 6.0 %fusion.31 = f32[2,2048,512]{1,2,0:T(8,128)S(1)} fusion(bf16[512,512,1]{0,1,2:T(8,128)(2,1)S(1)} %reshape.264, bf16[2]{0:T(256)(128)(2,1)S(1)} %get-tuple-element.198, bf16[2]{0:T(256)(128)(2,1)S(1)} %get-tuple-element.199, bf16[2]{0:T(256)(128)(2,1)S(1)} %get-tuple-element.200, bf16[2]{0:T(256)(128)(2,1)S(1)} %get-tuple-element.201, ...), kind=kOutput, calls=%fused_computation.52 | convolution fusion | flops 2183135232 | bytes 8929312 | tf_op jit(solution)/shard_map/dot_general | solution.py:124
  258.7 3.2 %fusion.34 = (f32[2,2048]{1,0:T(2,128)S(1)}, f32[2,2048]{1,0:T(2,128)S(1)}) fusion(f32[2,2048,512]{1,2,0:T(8,128)S(1)} %fusion.31, f32[2]{0:T(128)S(1)} %get-tuple-element.190, f32[2]{0:T(128)S(1)} %get-tuple-element.191, f32[2]{0:T(128)S(1)} %get-tuple-element.192, f32[2]{0:T(128)S(1)} %get-tuple-element.193, f32[2]{0:T(128)S(1)} %get-tuple-element.194, ...), kind=kLoop, calls=%fused_computation.56 | loop fusion | flops 22011904 | bytes 8437824 | tf_op jit(solution)/shard_map/reduce_sum | solution.py:68
  (203 shorter events, 102.4 us)
Async XLA Ops:
  6.5 227.0 %reduce-scatter.2.cloned.1.call-start = ((), (), s32[]{:S(2)}) async-start(), calls=%async_computation.2 | async-start | bytes 4456448 | tf_op jit(solution)/shard_map/reduce_scatter | solution.py:93
  158.0 0.8 copy-start
  158.0 0.8 copy-start.1
  158.0 81.1 %copy-start.2 = (s32[2]{0:T(128)S(1)}, s32[2]{0:T(128)}, u32[]{:S(2)}) copy-start(s32[2]{0:T(128)} %param.9) | copy-start | bytes 28
  235.7 16.5 %all-to-all-start = ((bf16[4,128,512]{1,2,0:T(8,128)(2,1)}), bf16[4,128,512]{1,2,0:T(8,128)(2,1)S(1)}, u32[]{:S(2)}, u32[]{:S(2)}) async-start(bf16[4,128,512]{1,2,0:T(8,128)(2,1)} %stack.16), calls=%async_computation.1 | async-start | bytes 1048576 | tf_op jit(solution)/shard_map/all_to_all | solution.py:108
Sparse Core Ops, SparseCore 0:
  158.2 75.2 reduce-scatter.1
